TPU v7x, 32 devices: a whole 2x2x4 slice. The times are simulated.
32 devices in a mesh: light: 8 (over z, y), depth: 2 (over core), tile: 2 (over x).
Axes of the slice: x: 2, y: 2, z: 4, core: 2. Of those that a mesh axis runs over, the one named last changes fastest.
Arguments:
- density: float32 [256, 128, 1024], P('light', 'depth', 'tile'), may hold values from 0.05 to 2
- extinction: float32 [3], replicated, may hold values from 1 to 4
- sun_colour: float32 [3], replicated, may hold values from 1 to 3
- sky_colour: float32 [3], replicated, may hold values from 0.2 to 2
Outputs:
- image: float32 [3, 256, 1024], P(None, ('light', 'depth'), 'tile')
- transmittance: float32 [3, 256, 1024], P(None, ('light', 'depth'), 'tile')
All inputs are finite; a program needn't handle non-finite values.
Results may differ from a plain program's by a relative error of at most 0.0003.
Values sent between devices are 32-bit elements; how exact they have to be, the bound alone decides.
A program may use at most 64 MiB of HBM per device.

v0:
```python
import jax
import jax.numpy as jnp
from jax import lax
from jax.sharding import PartitionSpec as P


def prefix(value, axis, combine, identity):
    size, position = (lax.axis_size(axis), lax.axis_index(axis))
    everything = lax.all_gather(value, axis)
    start = jnp.broadcast_to(jnp.asarray(identity, value.dtype), value.shape)

    def hop(k, before):
        reached = k < position
        new = combine(before, everything[k])
        return jnp.where(reached, new, before)

    return lax.fori_loop(0, size, hop, start)


def multiply_terms(earlier, later):
    return earlier * later


def per_device(density, extinction, sun_colour, sky_colour):
    light_count = lax.axis_size("light")
    depth_count = lax.axis_size("depth")
    full_x = density.shape[0] * light_count
    full_y = density.shape[1] * depth_count
    column_view = jnp.sum(density, axis=1)
    passing = jnp.exp(-extinction[:, None, None] * column_view[None] / full_y)
    front_all = prefix(passing, "depth", multiply_terms, jnp.ones_like(passing))
    front_pass = [front_all[colour] for colour in range(3)]
    column_light = jnp.sum(density, axis=0)
    own_index = lax.axis_index("light")
    piece = lax.all_gather(column_light[None], "light", axis=0, tiled=True)
    row_index = jnp.arange(piece.shape[0], dtype=jnp.int32)
    keep = (row_index < own_index)[:, None, None]
    before_light = jnp.sum(jnp.where(keep, piece, 0.0), axis=0)
    sun_depth = (before_light[None] + jnp.cumsum(density, axis=0) - 0.5 * density) / full_x
    local_view = (jnp.cumsum(density, axis=1) - density) / full_y
    shares = []
    for colour in range(3):
        radiance = sun_colour[colour] * jnp.exp(-extinction[colour] * sun_depth)
        opacity = -jnp.expm1(-extinction[colour] * density / full_y)
        weight = front_pass[colour][:, None, :] * jnp.exp(-extinction[colour] * local_view)
        shares.append(jnp.sum(weight * opacity * radiance, axis=1))
    contribution = jnp.stack(shares)
    summed, column_sum = (
        lax.psum_scatter(contribution, "depth", scatter_dimension=1, tiled=True),
        lax.psum_scatter(column_view[None], "depth", scatter_dimension=1, tiled=True),
    )
    transmittance = jnp.exp(-extinction[:, None, None] * column_sum / full_y)
    image = summed + sky_colour[:, None, None] * transmittance
    return (image, transmittance)


def solution(mesh):
    return jax.shard_map(
        per_device,
        mesh=mesh,
        in_specs=(P("light", "depth", "tile"), P(), P(), P()),
        out_specs=(P(None, ("light", "depth"), "tile"), P(None, ("light", "depth"), "tile")),
        check_vma=False,
    )
```

profile of v0, /device:TPU:25, one launch (start us, length us, event | category | flops | bytes accessed | tf_op | source)
XLA Modules:
  0.0 88.9 jit_solution(17001374396697318044)
XLA Ops:
  8.0 0.0 copy-start.1
  8.0 0.0 all-gather.3.cloned.1.call-start
  8.1 3.6 %fusion.3 = (f32[64,512]{1,0:T(8,128)}, f32[32,512]{1,0:T(8,128)}) fusion(f32[32,64,512]{2,1,0:T(8,128)} %param.6), kind=kLoop, calls=%fused_computation.18 | loop fusion | flops 2048000 | bytes 4390912 | tf_op jit(solution)/shard_map/reduce_sum | solution.py:33
  11.6 0.0 all-gather.3.cloned.1.call-update
  11.6 0.0 reduce-scatter.5.cloned.1.call-start
  11.7 0.5 reduce-scatter.5.cloned.1.call-update
  12.2 0.0 reduce-scatter.3.cloned.1.call-start
  12.3 0.0 copy-done.1
  12.3 0.6 fusion.5
  14.8 0.0 copy-start.2
  14.8 0.0 copy-start
  14.8 4.4 %fusion.6 = f32[32,64,512]{2,1,0:T(8,128)} fusion(f32[32,64,512]{2,1,0:T(8,128)} %param.6), kind=kOutput, calls=%fused_computation.21 | output fusion | flops 32505856 | bytes 8388608 | tf_op jit(solution)/shard_map/jit(cumsum)/reduce_window_sum | solution.py:39
  19.2 0.0 copy-done.2
  19.3 0.6 fusion.4
  19.9 0.0 copy-done
  19.9 0.1 multiply_exponential_fusion
  20.0 2.4 %all_gather.7 = f32[2,3,32,512]{3,2,1,0:T(8,128)S(1)} all-gather(f32[1,3,32,512]{3,2,1,0:T(8,128)S(1)} %multiply_exponential_fusion), channel_id=1, replica_groups=mesh['light'=8,'depth'=2,'tile'=2] {'depth'}, dimensions={0}, use_global_device_ids=true | all-gather | bytes 589824 | tf_op jit(solution)/shard_map/all_gather | solution.py:9
  22.4 0.2 while.14
  22.4 0.1 multiply_select_fusion.2
  22.4 0.1 multiply_select_fusion.2
  22.5 27.1 %all-gather.3.cloned.1.call-done = f32[512,512]{1,0:T(8,128)} async-done(((f32[64,512]{1,0:T(8,128)}), f32[512,512]{1,0:T(8,128)}) %all-gather.3.cloned.1.call-update) | async-done | bytes 1048592 | tf_op jit(solution)/shard_map/all_gather | solution.py:35
  49.7 1.4 %select_reduce_fusion = f32[64,512]{1,0:T(8,128)S(1)} fusion(f32[8,64,512]{2,1,0:T(8,128)} %bitcast.23, pred[8]{0:T(512)(128)(4,1)S(1)} %iota_compare_fusion), kind=kLoop, calls=%fused_computation.9 | loop fusion | flops 491520 | bytes 1179656 | tf_op jit(solution)/shard_map/reduce_sum | solution.py:38
  51.1 0.0 copy-start.3
  51.1 17.5 %multiply_reduce_fusion.2 = (f32[32,512]{1,0:T(8,128)S(1)}, f32[32,512]{1,0:T(8,128)S(1)}, f32[32,512]{1,0:T(8,128)S(1)}) fusion(f32[32,64,512]{2,1,0:T(8,128)} %param.6, f32[32,64,512]{2,1,0:T(8,128)} %fusion.6, f32[]{:T(128)S(6)} %mul.203, f32[64,512]{1,0:T(8,128)S(1)} %select_reduce_fusion, f32[]{:T(128)} %bitcast.2, f32[]{:T(128)} %bitcast.1, ...), kind=kOutput, calls=%fused_computation.5 | output fusion | flops 101662720 | bytes 8912944 | tf_op jit(solution)/shard_map/jit(cumsum)/reduce_window_sum | solution.py:40
  68.6 0.7 pad_maximum_fusion
  69.3 0.0 reduce-scatter.3.cloned.1.call-update
  69.3 0.0 reduce-scatter.5.cloned.1.call-done
  69.3 10.5 %reduce-scatter.3.cloned.1.call-done = f32[3,16,512]{2,1,0:T(8,128)} async-done(((f32[3,32,512]{2,1,0:T(8,128)}), f32[3,16,512]{2,1,0:T(8,128)}) %reduce-scatter.3.cloned.1.call-update) | async-done | bytes 98320 | tf_op jit(solution)/shard_map/reduce_scatter | solution.py:49
  79.8 0.0 copy-done.3
  79.8 1.7 %multiply_add_fusion = (f32[3,16,512]{2,1,0:T(8,128)}, f32[3,16,512]{2,1,0:T(8,128)}) fusion(f32[3,16,512]{2,1,0:T(8,128)} %reduce-scatter.3.cloned.1.call-done, f32[3]{0:T(128)S(1)} %copy-done.3, f32[16,512]{1,0:T(8,128)} %bitcast.28, f32[3]{0:T(128)S(1)} %neg.38), kind=kLoop, calls=%fused_computation.12 | loop fusion | flops 98304 | bytes 327704 | tf_op jit(solution)/shard_map/add | solution.py:53
  (4 shorter events, 0.0 us)
Async XLA Ops:
  8.0 4.3 %copy-start.1 = (f32[3]{0:T(128)S(1)}, f32[3]{0:T(128)}, u32[]{:S(2)}) copy-start(f32[3]{0:T(128)} %param.7) | copy-start | bytes 40
  8.0 41.7 %all-gather.3.cloned.1.call-start = ((), (), s32[]{:S(2)}) async-start(), calls=%async_computation.4 | async-start | bytes 1179648 | tf_op jit(solution)/shard_map/all_gather | solution.py:35
  11.6 57.7 %reduce-scatter.5.cloned.1.call-start = ((), (), s32[]{:S(2)}) async-start(), calls=%async_computation.3 | async-start | bytes 98304 | tf_op jit(solution)/shard_map/reduce_scatter | solution.py:50
  12.2 67.6 %reduce-scatter.3.cloned.1.call-start = ((), (), s32[]{:S(2)}) async-start(), calls=%async_computation.2 | async-start | bytes 294912 | tf_op jit(solution)/shard_map/reduce_scatter | solution.py:49
  14.8 4.5 %copy-start.2 = (f32[3]{0:T(128)S(1)}, f32[3]{0:T(128)}, u32[]{:S(2)}) copy-start(f32[3]{0:T(128)} %param.8) | copy-start | bytes 40
  14.8 5.1 %copy-start = (f32[32,512]{1,0:T(8,128)S(1)}, f32[32,512]{1,0:T(8,128)}, u32[]{:S(2)}) copy-start(f32[32,512]{1,0:T(8,128)} %get-tuple-element.101) | copy-start | bytes 196612
  51.1 28.7 %copy-start.3 = (f32[3]{0:T(128)S(1)}, f32[3]{0:T(128)}, u32[]{:S(2)}) copy-start(f32[3]{0:T(128)} %param.9) | copy-start | bytes 40
Sparse Core Ops, SparseCore 0:
  11.8 37.8 all-gather.2
Sparse Core Ops, SparseCore 1:
  14.9 9.2 reduce-scatter.4
  69.4 10.4 reduce-scatter.2
where the time goes:
time: 90.2 us; the launch traced here: 88.9 us
  waiting for transfers between devices  38.2 us (42%)
  other arithmetic  29.5 us (33%)
  between operations  17.5 us (19%)
  blocking collectives  2.39 us (3%)
  local copies, waits for them, and re-layouts  1.24 us (1%)
    all_gather x1, waiting for transfers between devices, per_device(): piece = lax.all_gather(column_light[None], 'light', axis=0, tiled=True)  27.1 us
    another operation x1, other arithmetic, per_device(): local_view = (jnp.cumsum(density, axis=1) - density) / full_y  17.5 us
    reduce_scatter x1, waiting for transfers between devices, per_device(): lax.psum_scatter(contribution, 'depth', scatter_dimension=1, tiled=True)  10.5 us
    another operation x1, other arithmetic, per_device(): jnp.cumsum(density, axis=0)  4.42 us
    reduce_sum x1, other arithmetic, per_device(): column_light = jnp.sum(density, axis=0)  3.56 us
    all_gather x1, blocking collectives, prefix(): everything = lax.all_gather(value, axis)  2.39 us
  transfers between devices with their start and end apart: 3, of which 2 were waited for; matrix products, arithmetic and copies ran while one was open for 29% of the time, Pallas kernels for 0%

commit v1 on v0

v1 whole, which is shorter than its diff:
```python
import functools
import math

import jax
import jax.numpy as jnp
from jax import lax
from jax.experimental import pallas as pl
from jax.experimental.pallas import tpu as pltpu
from jax.sharding import PartitionSpec as P

LANES = 128
ROWS = 8
LOG2E = math.log2(math.e)
MESH = pl.DeviceIdType.MESH


def kernel(light_count, full_x, full_y, density, extinction_in, sun_in, sky_in, image, trans,
           extinction, sun_colour, sky_colour, dens, weight, front, own, chain_in, side_in, before, share, share_in,
           small_sem, load_sem, chain_send, chain_recv, side_send, side_recv, share_send, share_recv):
    chunks, size_x, size_y, _ = dens.shape
    seg = size_y // ROWS
    half = size_x // 2
    pair = 2 if light_count % 2 == 0 else 1
    length = light_count // pair
    light = lax.axis_index("light")
    depth = lax.axis_index("depth")
    level, side = light // pair, light % pair
    last = level == length - 1
    partner = light + 1 - 2 * side
    other = 1 - depth

    sends_chain = level < length - 1
    gets_chain = level > 0
    if pair == 2:
        sends_side = jnp.logical_or(side == 0, level > 0)
        gets_side = jnp.logical_or(side == 1, level > 0)

    def load(j):
        return pltpu.make_async_copy(density.at[:, :, pl.ds(j * LANES, LANES)], dens.at[j], load_sem.at[j])

    def chain(j):
        return pltpu.make_async_remote_copy(
            own.at[j], chain_in.at[j], chain_send.at[j], chain_recv.at[j],
            device_id={"light": light + pair}, device_id_type=MESH)

    def side_copy(j, source):
        return pltpu.make_async_remote_copy(
            source.at[j], side_in.at[j], side_send.at[j], side_recv.at[j],
            device_id={"light": partner}, device_id_type=MESH)

    def share_copy(j):
        return pltpu.make_async_remote_copy(
            share.at[j, :, pl.ds(pl.multiple_of(other * half, half), half)], share_in.at[j],
            share_send.at[j], share_recv.at[j],
            device_id={"depth": other}, device_id_type=MESH)

    for j in range(chunks):
        load(j).start()
    colours = [pltpu.make_async_copy(a, b, small_sem.at[i]) for i, (a, b) in enumerate(
        ((extinction_in, extinction), (sun_in, sun_colour), (sky_in, sky_colour)))]
    for copy in colours:
        copy.start()

    barrier = pltpu.get_barrier_semaphore()
    pl.semaphore_signal(barrier, inc=1, device_id={"depth": other}, device_id_type=MESH)
    if pair == 2:
        pl.semaphore_signal(barrier, inc=1, device_id={"light": partner}, device_id_type=MESH)

    @pl.when(sends_chain)
    def _():
        pl.semaphore_signal(barrier, inc=1, device_id={"light": light + pair}, device_id_type=MESH)

    @pl.when(gets_chain)
    def _():
        pl.semaphore_signal(barrier, inc=1, device_id={"light": light - pair}, device_id_type=MESH)

    pl.semaphore_wait(barrier, pair + jnp.minimum(level, 1) + jnp.minimum(length - 1 - level, 1))

    def cells(j, x):
        return [dens[j, x, pl.ds(s, ROWS, stride=seg), :] for s in range(seg)]

    def send_sums(j):
        @pl.when(sends_chain)
        def _():
            chain(j).start()

        if pair == 2:
            @pl.when(side == 0)
            def _():
                side_copy(j, own).start()

    for j in range(chunks):
        load(j).wait()

        def sums(x, total):
            d = cells(j, x)
            front[j, x] = functools.reduce(jnp.add, d)
            return tuple(t + v for t, v in zip(total, d))

        zero = jnp.zeros((ROWS, LANES), jnp.float32)
        total = lax.fori_loop(0, size_x, sums, (zero,) * seg, unroll=4)
        for s in range(seg):
            own[j, s] = total[s]

        @pl.when(level == 0)
        def _():
            send_sums(j)

    row = lax.broadcasted_iota(jnp.int32, (ROWS, LANES), 0)

    def shifted(v, n):
        return jnp.where(row >= n, pltpu.roll(v, n, 0), 0.0)

    def scan_group(g, carry):
        j, b = g // (size_x // ROWS), g % (size_x // ROWS)
        x0 = pl.multiple_of(b * ROWS, ROWS)
        group = front[j, pl.ds(x0, ROWS)]
        share[j, 3, pl.ds(x0, ROWS)] = jnp.sum(group, axis=1)
        for i in range(ROWS):
            v = shifted(group[i], 1)
            n = 1
            while n < ROWS:
                v = v + shifted(v, n)
                n *= 2
            front[j, x0 + i] = v
        return carry

    lax.fori_loop(0, chunks * (size_x // ROWS), scan_group, 0)

    for copy in colours:
        copy.wait()
    half_step = [extinction[c] * (-LOG2E / (2 * full_x)) for c in range(3)]
    view_step = [extinction[c] * (-LOG2E / full_y) for c in range(3)]
    sun_step = [extinction[c] * (-LOG2E / full_x) for c in range(3)]
    ratio = 2 * full_x // full_y
    squares = ratio.bit_length() - 1
    by_squares = ratio * full_y == 2 * full_x and ratio == 1 << squares and squares <= 3

    def weigh(j, carry):
        def step(x, lit):
            d = cells(j, x)
            e = front[j, x]
            after = []
            for c in range(3):
                seen = jnp.exp2(view_step[c] * e)
                for s in range(seg):
                    q = jnp.exp2(half_step[c] * d[s])
                    if by_squares:
                        a = q
                        for _ in range(squares):
                            a = a * a
                    else:
                        a = jnp.exp2(view_step[c] * d[s])
                    r = lit[c * seg + s] * q
                    after.append(r * q)
                    behind = seen * a
                    weight[j, c, x, s] = (seen - behind) * r
                    seen = behind
            return tuple(after)

        one = jnp.ones((ROWS, LANES), jnp.float32)
        lax.fori_loop(0, size_x, step, (one,) * (3 * seg))
        return carry

    early = jnp.minimum(level, chunks)
    lax.fori_loop(0, early, weigh, 0)

    for j in range(chunks):
        @pl.when(gets_chain)
        def _():
            chain(j).wait_recv()
            if pair == 2:
                @pl.when(side == 1)
                def _():
                    side_copy(j, chain_in).start()
            own[j] = own[j] + chain_in[j]
            send_sums(j)

    lax.fori_loop(early, chunks, weigh, 0)

    def finish_rows(j, block):
        for c in range(3):
            g = [sun_colour[c] * jnp.exp2(sun_step[c] * before[s]) for s in range(seg)]
            for b in range(half // ROWS):
                x0 = block * half + b * ROWS
                parts = []
                for i in range(ROWS):
                    acc = weight[j, c, x0 + i, 0] * g[0]
                    for s in range(1, seg):
                        acc = acc + weight[j, c, x0 + i, s] * g[s]
                    parts.append(acc)
                share[j, c, pl.ds(pl.multiple_of(x0, ROWS), ROWS)] = jnp.sum(jnp.stack(parts), axis=1)

    def prepare(j):
        before[...] = jnp.zeros_like(before)

        @pl.when(gets_chain)
        def _():
            before[...] = chain_in[j]

        if pair == 2:
            @pl.when(gets_side)
            def _():
                side_copy(j, own).wait_recv()
                before[...] = before[...] + side_in[j]

    def combine(j):
        share_copy(j).wait_recv()
        mine = pl.ds(pl.multiple_of(depth * half, half), half)
        lanes = pl.ds(j * LANES, LANES)
        near = depth == 0
        view, view_in = share[j, 3, mine], share_in[j, 3]
        view_front = jnp.where(near, view, view_in)
        for c in range(3):
            here, there = share[j, c, mine], share_in[j, c]
            first, second = jnp.where(near, here, there), jnp.where(near, there, here)
            passing = jnp.exp2(view_step[c] * (view + view_in))
            trans[c, :, lanes] = passing
            image[c, :, lanes] = (first + jnp.exp2(view_step[c] * view_front) * second) + sky_colour[c] * passing

    for j in range(chunks):
        prepare(j)
        finish_rows(j, other)
        share_copy(j).start()
        finish_rows(j, depth)
    for j in range(chunks):
        combine(j)

    for j in range(chunks):
        share_copy(j).wait_send()

        @pl.when(sends_chain)
        def _():
            chain(j).wait_send()

        if pair == 2:
            @pl.when(sends_side)
            def _():
                side_copy(j, own).wait_send()


def per_device(mesh_shape, density, extinction, sun_colour, sky_colour):
    light_count, depth_count = mesh_shape["light"], mesh_shape["depth"]
    size_x, size_y, size_z = density.shape
    assert depth_count == 2
    chunks, seg, half = size_z // LANES, size_y // ROWS, size_x // 2
    out = jax.ShapeDtypeStruct((3, half, size_z), jnp.float32)
    vmem = functools.partial(pltpu.VMEM, dtype=jnp.float32)
    tile = (ROWS, LANES)
    dma = pltpu.SemaphoreType.DMA((chunks,))
    hbm = pl.BlockSpec(memory_space=pltpu.HBM)
    small = pltpu.SMEM((3,), jnp.float32)
    whole = pl.BlockSpec(memory_space=pltpu.VMEM)
    return pl.pallas_call(
        functools.partial(kernel, light_count, size_x * light_count, size_y * depth_count),
        out_shape=(out, out),
        in_specs=[hbm] * 4,
        out_specs=(whole, whole),
        scratch_shapes=[small] * 3 + [
            vmem((chunks, size_x, size_y, LANES)),
            vmem((chunks, 3, size_x, seg) + tile),
            vmem((chunks, size_x) + tile),
            vmem((chunks, seg) + tile),
            vmem((chunks, seg) + tile),
            vmem((chunks, seg) + tile),
            vmem((seg,) + tile),
            vmem((chunks, 4, size_x, LANES)),
            vmem((chunks, 4, half, LANES)),
        ] + [pltpu.SemaphoreType.DMA((3,))] + [dma] * 7,
        compiler_params=pltpu.CompilerParams(collective_id=0, has_side_effects=True, vmem_limit_bytes=48 * 2**20),
    )(density, extinction, sun_colour, sky_colour)


def solution(mesh):
    return jax.shard_map(
        functools.partial(per_device, dict(mesh.shape)),
        mesh=mesh,
        in_specs=(P("light", "depth", "tile"), P(), P(), P()),
        out_specs=(P(None, ("light", "depth"), "tile"), P(None, ("light", "depth"), "tile")),
        check_vma=False,
    )
```

time: 90.2 us -> 22.5 us (0.25); the launches traced: 88.9 us -> 22.3 us
  waiting for transfers between devices: 38.2 us -> 0 us
  other arithmetic: 29.5 us -> 0 us
  between operations: 17.5 us -> 0.65 us
  Pallas kernels: 0 us -> 16.2 us
  local copies, waits for them, and re-layouts: 1.24 us -> 5.43 us
  blocking collectives: 2.39 us -> 0 us
    all_gather x1 -> x0, waiting for transfers between devices: 27.1 us -> none  [per_device(): piece = lax.all_gather(column_light[None], 'light', axis=0, tiled=True)]
    another operation x3 -> x0, other arithmetic: 22.6 us -> none  [the longest x1 17.5 us: per_device(): local_view = (jnp.cumsum(density, axis=1) - density) / full_y]
    pallas_call x0 -> x1, Pallas kernels: none -> 16.2 us  [per_device(): pl.pallas_call(functools.partial(kernel, light_count, size_x * light_coun...]
    reduce_scatter x2 -> x0, waiting for transfers between devices: 10.5 us -> none  [the longest x1 10.5 us: per_device(): lax.psum_scatter(contribution, 'depth', scatter_dimension=1, tiled=True)]
    unnamed x8 -> x10, local copies, waits for them, and re-layouts: 0.02 us -> 5.43 us
    reduce_sum x2 -> x0, other arithmetic: 4.96 us -> none  [the longest x1 3.56 us: per_device(): column_light = jnp.sum(density, axis=0)]
    all_gather x1 -> x0, blocking collectives: 2.39 us -> none  [prefix(): everything = lax.all_gather(value, axis)]
    add x1 -> x0, other arithmetic: 1.66 us -> none  [per_device(): image = summed + sky_colour[:, None, None] * transmittance]
  transfers between devices with their start and end apart: 3 -> 0, of which waited for: 2 -> 0; matrix products, arithmetic and copies ran while one was open for 29% -> 0% of each run, Pallas kernels for 0% -> 0%
where the time goes in v1:
time: 22.5 us; the launch traced here: 22.3 us
  Pallas kernels  16.2 us (72%)
  local copies, waits for them, and re-layouts  5.43 us (24%)
  between operations  0.65 us (3%)
    pallas_call x1, Pallas kernels, per_device(): pl.pallas_call(functools.partial(kernel, light_count, size_x * light_coun...  16.2 us
    unnamed x10, local copies, waits for them, and re-layouts  5.43 us

profile of v1, /device:TPU:25, one launch (start us, length us, event | category | flops | bytes accessed | tf_op | source)
XLA Modules:
  0.0 22.3 jit_solution(16473917463255837843)
XLA Ops:
  0.6 0.0 copy-start
  0.6 2.2 %copy-done = f32[32,64,512]{2,1,0:T(8,128)S(1)} copy-done((f32[32,64,512]{2,1,0:T(8,128)S(1)}, f32[32,64,512]{2,1,0:T(8,128)}, u32[]{:S(2)}) %copy-start) | copy-done | bytes 4194328
  2.8 0.0 copy-start.1
  2.8 0.7 %copy-done.1 = f32[3]{0:T(128)S(1)} copy-done((f32[3]{0:T(128)S(1)}, f32[3]{0:T(128)}, u32[]{:S(2)}) %copy-start.1) | copy-done | bytes 36
  3.5 0.0 copy-start.2
  3.5 0.7 %copy-done.2 = f32[3]{0:T(128)S(1)} copy-done((f32[3]{0:T(128)S(1)}, f32[3]{0:T(128)}, u32[]{:S(2)}) %copy-start.2) | copy-done | bytes 36
  4.1 0.0 copy-start.3
  4.1 0.7 %copy-done.3 = f32[3]{0:T(128)S(1)} copy-done((f32[3]{0:T(128)S(1)}, f32[3]{0:T(128)}, u32[]{:S(2)}) %copy-start.3) | copy-done | bytes 36
  4.8 16.2 %shard_map.59 = (f32[3,16,512]{2,1,0:T(8,128)S(1)}, f32[3,16,512]{2,1,0:T(8,128)S(1)}) custom-call(f32[32,64,512]{2,1,0:T(8,128)S(1)} %copy-done, f32[3]{0:T(128)S(1)} %copy-done.1, f32[3]{0:T(128)S(1)} %copy-done.2, f32[3]{0:T(128)S(1)} %copy-done.3), custom_call_target="tpu_custom_call" | custom-call | tf_op jit(solution)/shard_map/pallas_call | solution.py:254
  21.0 0.6 %copy.8 = f32[3,16,512]{2,1,0:T(8,128)} copy(f32[3,16,512]{2,1,0:T(8,128)S(1)} %get-tuple-element.4) | data formatting | bytes 196608
  21.6 0.6 %copy.9 = f32[3,16,512]{2,1,0:T(8,128)} copy(f32[3,16,512]{2,1,0:T(8,128)S(1)} %get-tuple-element.5) | data formatting | bytes 196608
Async XLA Ops:
  0.6 2.2 %copy-start = (f32[32,64,512]{2,1,0:T(8,128)S(1)}, f32[32,64,512]{2,1,0:T(8,128)}, u32[]{:S(2)}) copy-start(f32[32,64,512]{2,1,0:T(8,128)} %density.1) | copy-start | bytes 12582916
  2.8 0.7 %copy-start.1 = (f32[3]{0:T(128)S(1)}, f32[3]{0:T(128)}, u32[]{:S(2)}) copy-start(f32[3]{0:T(128)} %extinction_in.1) | copy-start | bytes 40
  3.5 0.7 %copy-start.2 = (f32[3]{0:T(128)S(1)}, f32[3]{0:T(128)}, u32[]{:S(2)}) copy-start(f32[3]{0:T(128)} %sun_in.1) | copy-start | bytes 40
  4.1 0.7 %copy-start.3 = (f32[3]{0:T(128)S(1)}, f32[3]{0:T(128)}, u32[]{:S(2)}) copy-start(f32[3]{0:T(128)} %sky_in.1) | copy-start | bytes 40

commit v2 on v1

--- a/solution.py
+++ b/solution.py
@@ -14,8 +14,8 @@
 MESH = pl.DeviceIdType.MESH
 
 
-def kernel(light_count, full_x, full_y, density, extinction_in, sun_in, sky_in, image, trans,
-           extinction, sun_colour, sky_colour, dens, weight, front, own, chain_in, side_in, before, share, share_in,
+def kernel(light_count, full_x, full_y, density, extinction_in, sun_in, image, column,
+           extinction, sun_colour, dens, weight, front, own, chain_in, side_in, before, share, share_in,
            small_sem, load_sem, chain_send, chain_recv, side_send, side_recv, share_send, share_recv):
     chunks, size_x, size_y, _ = dens.shape
     seg = size_y // ROWS
@@ -57,7 +57,7 @@
     for j in range(chunks):
         load(j).start()
     colours = [pltpu.make_async_copy(a, b, small_sem.at[i]) for i, (a, b) in enumerate(
-        ((extinction_in, extinction), (sun_in, sun_colour), (sky_in, sky_colour)))]
+        ((extinction_in, extinction), (sun_in, sun_colour)))]
     for copy in colours:
         copy.start()
 
@@ -214,9 +214,8 @@
         for c in range(3):
             here, there = share[j, c, mine], share_in[j, c]
             first, second = jnp.where(near, here, there), jnp.where(near, there, here)
-            passing = jnp.exp2(view_step[c] * (view + view_in))
-            trans[c, :, lanes] = passing
-            image[c, :, lanes] = (first + jnp.exp2(view_step[c] * view_front) * second) + sky_colour[c] * passing
+            image[c, :, lanes] = first + jnp.exp2(view_step[c] * view_front) * second
+        column[:, lanes] = view + view_in
 
     for j in range(chunks):
         prepare(j)
@@ -251,12 +250,12 @@
     hbm = pl.BlockSpec(memory_space=pltpu.HBM)
     small = pltpu.SMEM((3,), jnp.float32)
     whole = pl.BlockSpec(memory_space=pltpu.VMEM)
-    return pl.pallas_call(
+    image, column = pl.pallas_call(
         functools.partial(kernel, light_count, size_x * light_count, size_y * depth_count),
-        out_shape=(out, out),
-        in_specs=[hbm] * 4,
+        out_shape=(out, jax.ShapeDtypeStruct((half, size_z), jnp.float32)),
+        in_specs=[hbm] * 3,
         out_specs=(whole, whole),
-        scratch_shapes=[small] * 3 + [
+        scratch_shapes=[small] * 2 + [
             vmem((chunks, size_x, size_y, LANES)),
             vmem((chunks, 3, size_x, seg) + tile),
             vmem((chunks, size_x) + tile),
@@ -266,9 +265,11 @@
             vmem((seg,) + tile),
             vmem((chunks, 4, size_x, LANES)),
             vmem((chunks, 4, half, LANES)),
-        ] + [pltpu.SemaphoreType.DMA((3,))] + [dma] * 7,
-        compiler_params=pltpu.CompilerParams(collective_id=0, has_side_effects=True, vmem_limit_bytes=48 * 2**20),
-    )(density, extinction, sun_colour, sky_colour)
+        ] + [pltpu.SemaphoreType.DMA((2,))] + [dma] * 7,
+        compiler_params=pltpu.CompilerParams(collective_id=0, has_side_effects=True, vmem_limit_bytes=67043328),
+    )(density, extinction, sun_colour)
+    trans = jnp.exp(extinction[:, None, None] * (column / -(size_y * depth_count)))
+    return image + sky_colour[:, None, None] * trans, trans
 
 
 def solution(mesh):

time: 22.5 us -> 19.9 us (0.88)
  local copies, waits for them, and re-layouts: 5.43 us -> 0 us
  other arithmetic: 0 us -> 2.44 us
  Pallas kernels: 16.2 us -> 16.6 us
    unnamed x10 -> x0, local copies, waits for them, and re-layouts: 5.43 us -> none
    add x0 -> x1, other arithmetic: none -> 1.67 us  [per_device(): return (image + sky_colour[:, None, None] * trans, trans)]
    div x0 -> x1, other arithmetic: none -> 0.76 us  [per_device(): column / -(size_y * depth_count)]
    pallas_call x1, Pallas kernels: 16.2 us -> 16.6 us  [per_device(): pl.pallas_call(functools.partial(kernel, light_count, size_x * light_coun...]
where the time goes in v2:
time: 19.9 us; the launch traced here: 19.6 us
  Pallas kernels  16.6 us (83%)
  other arithmetic  2.44 us (12%)
  between operations  0.64 us (3%)
    pallas_call x1, Pallas kernels, per_device(): pl.pallas_call(functools.partial(kernel, light_count, size_x * light_coun...  16.6 us
    add x1, other arithmetic, per_device(): return (image + sky_colour[:, None, None] * trans, trans)  1.67 us
    div x1, other arithmetic, per_device(): column / -(size_y * depth_count)  0.76 us

profile of v2, /device:TPU:25, one launch (start us, length us, event | category | flops | bytes accessed | tf_op | source)
XLA Modules:
  0.0 19.6 jit_solution(7206411382644941394)
XLA Ops:
  0.6 16.6 %shard_map.59 = (f32[3,16,512]{2,1,0:T(8,128)}, f32[16,512]{1,0:T(8,128)}) custom-call(f32[32,64,512]{2,1,0:T(8,128)} %density.1, f32[3]{0:T(128)} %extinction_in.1, f32[3]{0:T(128)} %sun_in.1), custom_call_target="tpu_custom_call" | custom-call | tf_op jit(solution)/shard_map/pallas_call | solution.py:253
  17.2 0.8 %broadcast_multiply_fusion = f32[16,512]{1,0:T(8,128)S(1)} fusion(f32[16,512]{1,0:T(8,128)} %get-tuple-element.5), kind=kLoop, calls=%fused_computation.2 | loop fusion | flops 8192 | bytes 65536 | tf_op jit(solution)/shard_map/div | solution.py:271
  18.0 1.7 %multiply_add_fusion = (f32[3,16,512]{2,1,0:T(8,128)}, f32[3,16,512]{2,1,0:T(8,128)}) fusion(f32[3,16,512]{2,1,0:T(8,128)} %get-tuple-element.4, f32[3]{0:T(128)} %param.7, f32[16,512]{1,0:T(8,128)S(1)} %broadcast_multiply_fusion, f32[3]{0:T(128)} %extinction_in.1), kind=kLoop, calls=%fused_computation | loop fusion | flops 73728 | bytes 327704 | tf_op jit(solution)/shard_map/add | solution.py:272

commit v3 on v2

--- a/solution.py
+++ b/solution.py
@@ -159,7 +159,7 @@
             return tuple(after)
 
         one = jnp.ones((ROWS, LANES), jnp.float32)
-        lax.fori_loop(0, size_x, step, (one,) * (3 * seg))
+        lax.fori_loop(0, size_x, step, (one,) * (3 * seg), unroll=2)
         return carry
 
     early = jnp.minimum(level, chunks)
@@ -215,7 +215,7 @@
             here, there = share[j, c, mine], share_in[j, c]
             first, second = jnp.where(near, here, there), jnp.where(near, there, here)
             image[c, :, lanes] = first + jnp.exp2(view_step[c] * view_front) * second
-        column[:, lanes] = view + view_in
+        column[:, lanes] = (view + view_in) * (-1.0 / full_y)
 
     for j in range(chunks):
         prepare(j)
@@ -266,9 +266,9 @@
             vmem((chunks, 4, size_x, LANES)),
             vmem((chunks, 4, half, LANES)),
         ] + [pltpu.SemaphoreType.DMA((2,))] + [dma] * 7,
-        compiler_params=pltpu.CompilerParams(collective_id=0, has_side_effects=True, vmem_limit_bytes=67043328),
-    )(density, extinction, sun_colour)
-    trans = jnp.exp(extinction[:, None, None] * (column / -(size_y * depth_count)))
+        compiler_params=pltpu.CompilerParams(collective_id=0, has_side_effects=True, vmem_limit_bytes=48 * 2**20),
+    )(*[pltpu.with_memory_space_constraint(a, pltpu.HBM) for a in (density, extinction, sun_colour)])
+    trans = jnp.exp(extinction[:, None, None] * column)
     return image + sky_colour[:, None, None] * trans, trans
 
 

time: 19.9 us -> 17.3 us (0.87)
  other arithmetic: 2.44 us -> 0.76 us
  Pallas kernels: 16.6 us -> 15.7 us
    add x1, other arithmetic: 1.67 us -> 0.76 us  [per_device(): return (image + sky_colour[:, None, None] * trans, trans)]
    pallas_call x1, Pallas kernels: 16.6 us -> 15.7 us  [per_device(): pl.pallas_call(functools.partial(kernel, light_count, size_x * light_coun...]
    div x1 -> x0, other arithmetic: 0.76 us -> none  [per_device(): column / -(size_y * depth_count)]
where the time goes in v3:
time: 17.3 us; the launch traced here: 17.2 us
  Pallas kernels  15.7 us (91%)
  other arithmetic  0.76 us (4%)
  between operations  0.67 us (4%)
    pallas_call x1, Pallas kernels, per_device(): pl.pallas_call(functools.partial(kernel, light_count, size_x * light_coun...  15.7 us
    add x1, other arithmetic, per_device(): return (image + sky_colour[:, None, None] * trans, trans)  0.76 us

profile of v3, /device:TPU:25, one launch (start us, length us, event | category | flops | bytes accessed | tf_op | source)
XLA Modules:
  0.0 17.2 jit_solution(15736353754699064880)
XLA Ops:
  0.6 0.0 copy-start
  0.6 0.0 copy-start.1
  0.7 15.7 %shard_map.59 = (f32[3,16,512]{2,1,0:T(8,128)S(1)}, f32[16,512]{1,0:T(8,128)S(1)}) custom-call(f32[32,64,512]{2,1,0:T(8,128)} %density.1, f32[3]{0:T(128)} %extinction_in.1, f32[3]{0:T(128)} %sun_in.1), custom_call_target="tpu_custom_call" | custom-call | tf_op jit(solution)/shard_map/pallas_call | solution.py:253
  16.4 0.0 copy-done
  16.4 0.0 copy-done.1
  16.4 0.8 %multiply_add_fusion = (f32[3,16,512]{2,1,0:T(8,128)}, f32[3,16,512]{2,1,0:T(8,128)}) fusion(f32[3,16,512]{2,1,0:T(8,128)S(1)} %get-tuple-element.4, f32[3]{0:T(128)S(1)} %copy-done.1, f32[16,512]{1,0:T(8,128)S(1)} %get-tuple-element.5, f32[3]{0:T(128)S(1)} %copy-done), kind=kLoop, calls=%fused_computation | loop fusion | flops 73728 | bytes 327704 | tf_op jit(solution)/shard_map/add | solution.py:272
Async XLA Ops:
  0.6 15.8 %copy-start = (f32[3]{0:T(128)S(1)}, f32[3]{0:T(128)}, u32[]{:S(2)}) copy-start(f32[3]{0:T(128)} %extinction_in.1) | copy-start | bytes 40
  0.6 15.8 %copy-start.1 = (f32[3]{0:T(128)S(1)}, f32[3]{0:T(128)}, u32[]{:S(2)}) copy-start(f32[3]{0:T(128)} %param.7) | copy-start | bytes 40

commit v4 on v3

--- a/solution.py
+++ b/solution.py
@@ -9,6 +9,7 @@
 from jax.sharding import PartitionSpec as P
 
 LANES = 128
+PARTS = 4
 ROWS = 8
 LOG2E = math.log2(math.e)
 MESH = pl.DeviceIdType.MESH
@@ -38,14 +39,22 @@
     def load(j):
         return pltpu.make_async_copy(density.at[:, :, pl.ds(j * LANES, LANES)], dens.at[j], load_sem.at[j])
 
-    def chain(j):
+    part = seg // PARTS
+    messages = [(j, p) for j in range(chunks) for p in range(PARTS)]
+
+    def steps(m):
+        return m[0], pl.ds(m[1] * part, part)
+
+    def chain(m):
+        n = m[0] * PARTS + m[1]
         return pltpu.make_async_remote_copy(
-            own.at[j], chain_in.at[j], chain_send.at[j], chain_recv.at[j],
+            own.at[steps(m)], chain_in.at[steps(m)], chain_send.at[n], chain_recv.at[n],
             device_id={"light": light + pair}, device_id_type=MESH)
 
-    def side_copy(j, source):
+    def side_copy(m, source):
+        n = m[0] * PARTS + m[1]
         return pltpu.make_async_remote_copy(
-            source.at[j], side_in.at[j], side_send.at[j], side_recv.at[j],
+            source.at[steps(m)], side_in.at[steps(m)], side_send.at[n], side_recv.at[n],
             device_id={"light": partner}, device_id_type=MESH)
 
     def share_copy(j):
@@ -79,15 +88,15 @@
     def cells(j, x):
         return [dens[j, x, pl.ds(s, ROWS, stride=seg), :] for s in range(seg)]
 
-    def send_sums(j):
+    def send_sums(m):
         @pl.when(sends_chain)
         def _():
-            chain(j).start()
+            chain(m).start()
 
         if pair == 2:
             @pl.when(side == 0)
             def _():
-                side_copy(j, own).start()
+                side_copy(m, own).start()
 
     for j in range(chunks):
         load(j).wait()
@@ -104,7 +113,8 @@
 
         @pl.when(level == 0)
         def _():
-            send_sums(j)
+            for p in range(PARTS):
+                send_sums((j, p))
 
     row = lax.broadcasted_iota(jnp.int32, (ROWS, LANES), 0)
 
@@ -162,19 +172,19 @@
         lax.fori_loop(0, size_x, step, (one,) * (3 * seg), unroll=2)
         return carry
 
-    early = jnp.minimum(level, chunks)
+    early = jnp.minimum(level * chunks // max(length - 1, 1), chunks)
     lax.fori_loop(0, early, weigh, 0)
 
-    for j in range(chunks):
-        @pl.when(gets_chain)
-        def _():
-            chain(j).wait_recv()
+    @pl.when(gets_chain)
+    def _():
+        for m in messages:
+            chain(m).wait_recv()
             if pair == 2:
                 @pl.when(side == 1)
                 def _():
-                    side_copy(j, chain_in).start()
-            own[j] = own[j] + chain_in[j]
-            send_sums(j)
+                    side_copy(m, chain_in).start()
+            own[steps(m)] = own[steps(m)] + chain_in[steps(m)]
+            send_sums(m)
 
     lax.fori_loop(early, chunks, weigh, 0)
 
@@ -201,7 +211,8 @@
         if pair == 2:
             @pl.when(gets_side)
             def _():
-                side_copy(j, own).wait_recv()
+                for p in range(PARTS):
+                    side_copy((j, p), own).wait_recv()
                 before[...] = before[...] + side_in[j]
 
     def combine(j):
@@ -228,14 +239,16 @@
     for j in range(chunks):
         share_copy(j).wait_send()
 
-        @pl.when(sends_chain)
-        def _():
-            chain(j).wait_send()
-
-        if pair == 2:
-            @pl.when(sends_side)
-            def _():
-                side_copy(j, own).wait_send()
+    @pl.when(sends_chain)
+    def _():
+        for m in messages:
+            chain(m).wait_send()
+
+    if pair == 2:
+        @pl.when(sends_side)
+        def _():
+            for m in messages:
+                side_copy(m, own).wait_send()
 
 
 def per_device(mesh_shape, density, extinction, sun_colour, sky_colour):
@@ -247,6 +260,7 @@
     vmem = functools.partial(pltpu.VMEM, dtype=jnp.float32)
     tile = (ROWS, LANES)
     dma = pltpu.SemaphoreType.DMA((chunks,))
+    message = pltpu.SemaphoreType.DMA((chunks * PARTS,))
     hbm = pl.BlockSpec(memory_space=pltpu.HBM)
     small = pltpu.SMEM((3,), jnp.float32)
     whole = pl.BlockSpec(memory_space=pltpu.VMEM)
@@ -265,7 +279,7 @@
             vmem((seg,) + tile),
             vmem((chunks, 4, size_x, LANES)),
             vmem((chunks, 4, half, LANES)),
-        ] + [pltpu.SemaphoreType.DMA((2,))] + [dma] * 7,
+        ] + [pltpu.SemaphoreType.DMA((2,))] + [dma] + [message] * 4 + [dma] * 2,
         compiler_params=pltpu.CompilerParams(collective_id=0, has_side_effects=True, vmem_limit_bytes=48 * 2**20),
     )(*[pltpu.with_memory_space_constraint(a, pltpu.HBM) for a in (density, extinction, sun_colour)])
     trans = jnp.exp(extinction[:, None, None] * column)

time: 17.3 us -> 17.3 us (level)
  no operation moved by 1% of the time
where the time goes in v4:
time: 17.3 us; the launch traced here: 17.1 us
  Pallas kernels  15.7 us (91%)
  other arithmetic  0.76 us (4%)
  between operations  0.67 us (4%)
    pallas_call x1, Pallas kernels, per_device(): pl.pallas_call(functools.partial(kernel, light_count, size_x * light_coun...  15.7 us
    add x1, other arithmetic, per_device(): return (image + sky_colour[:, None, None] * trans, trans)  0.76 us

profile of v4, /device:TPU:25, one launch (start us, length us, event | category | flops | bytes accessed | tf_op | source)
XLA Modules:
  0.0 17.1 jit_solution(18027847499996659568)
XLA Ops:
  0.6 0.0 copy-start
  0.6 0.0 copy-start.1
  0.7 15.7 %shard_map.59 = (f32[3,16,512]{2,1,0:T(8,128)S(1)}, f32[16,512]{1,0:T(8,128)S(1)}) custom-call(f32[32,64,512]{2,1,0:T(8,128)} %density.1, f32[3]{0:T(128)} %extinction_in.1, f32[3]{0:T(128)} %sun_in.1), custom_call_target="tpu_custom_call" | custom-call | tf_op jit(solution)/shard_map/pallas_call | solution.py:267
  16.3 0.0 copy-done
  16.3 0.0 copy-done.1
  16.3 0.8 %multiply_add_fusion = (f32[3,16,512]{2,1,0:T(8,128)}, f32[3,16,512]{2,1,0:T(8,128)}) fusion(f32[3,16,512]{2,1,0:T(8,128)S(1)} %get-tuple-element.4, f32[3]{0:T(128)S(1)} %copy-done.1, f32[16,512]{1,0:T(8,128)S(1)} %get-tuple-element.5, f32[3]{0:T(128)S(1)} %copy-done), kind=kLoop, calls=%fused_computation | loop fusion | flops 73728 | bytes 327704 | tf_op jit(solution)/shard_map/add | solution.py:286
Async XLA Ops:
  0.6 15.7 %copy-start = (f32[3]{0:T(128)S(1)}, f32[3]{0:T(128)}, u32[]{:S(2)}) copy-start(f32[3]{0:T(128)} %extinction_in.1) | copy-start | bytes 40
  0.6 15.7 %copy-start.1 = (f32[3]{0:T(128)S(1)}, f32[3]{0:T(128)}, u32[]{:S(2)}) copy-start(f32[3]{0:T(128)} %param.7) | copy-start | bytes 40

commit v5 on v4

--- a/solution.py
+++ b/solution.py
@@ -9,7 +9,7 @@
 from jax.sharding import PartitionSpec as P
 
 LANES = 128
-PARTS = 4
+PARTS = 2
 ROWS = 8
 LOG2E = math.log2(math.e)
 MESH = pl.DeviceIdType.MESH
@@ -135,7 +135,7 @@
             front[j, x0 + i] = v
         return carry
 
-    lax.fori_loop(0, chunks * (size_x // ROWS), scan_group, 0)
+    lax.fori_loop(0, chunks * (size_x // ROWS), scan_group, 0, unroll=4)
 
     for copy in colours:
         copy.wait()
@@ -147,12 +147,12 @@
     by_squares = ratio * full_y == 2 * full_x and ratio == 1 << squares and squares <= 3
 
     def weigh(j, carry):
-        def step(x, lit):
-            d = cells(j, x)
-            e = front[j, x]
-            after = []
-            for c in range(3):
-                seen = jnp.exp2(view_step[c] * e)
+        one = jnp.ones((ROWS, LANES), jnp.float32)
+        for c in range(3):
+            def step(x, lit):
+                d = cells(j, x)
+                seen = jnp.exp2(view_step[c] * front[j, x])
+                after = []
                 for s in range(seg):
                     q = jnp.exp2(half_step[c] * d[s])
                     if by_squares:
@@ -161,15 +161,14 @@
                             a = a * a
                     else:
                         a = jnp.exp2(view_step[c] * d[s])
-                    r = lit[c * seg + s] * q
+                    r = lit[s] * q
                     after.append(r * q)
                     behind = seen * a
                     weight[j, c, x, s] = (seen - behind) * r
                     seen = behind
-            return tuple(after)
-
-        one = jnp.ones((ROWS, LANES), jnp.float32)
-        lax.fori_loop(0, size_x, step, (one,) * (3 * seg), unroll=2)
+                return tuple(after)
+
+            lax.fori_loop(0, size_x, step, (one,) * seg, unroll=4)
         return carry
 
     early = jnp.minimum(level * chunks // max(length - 1, 1), chunks)

time: 17.3 us -> 17.2 us (level)
  no operation moved by 1% of the time
where the time goes in v5:
time: 17.2 us; the launch traced here: 17.1 us
  Pallas kernels  15.6 us (91%)
  other arithmetic  0.76 us (4%)
  between operations  0.67 us (4%)
    pallas_call x1, Pallas kernels, per_device(): pl.pallas_call(functools.partial(kernel, light_count, size_x * light_coun...  15.6 us
    add x1, other arithmetic, per_device(): return (image + sky_colour[:, None, None] * trans, trans)  0.76 us

profile of v5, /device:TPU:25, one launch (start us, length us, event | category | flops | bytes accessed | tf_op | source)
XLA Modules:
  0.0 17.1 jit_solution(6024743623720157319)
XLA Ops:
  0.6 0.0 copy-start
  0.6 0.0 copy-start.1
  0.7 15.6 %shard_map.59 = (f32[3,16,512]{2,1,0:T(8,128)S(1)}, f32[16,512]{1,0:T(8,128)S(1)}) custom-call(f32[32,64,512]{2,1,0:T(8,128)} %density.1, f32[3]{0:T(128)} %extinction_in.1, f32[3]{0:T(128)} %sun_in.1), custom_call_target="tpu_custom_call" | custom-call | tf_op jit(solution)/shard_map/pallas_call | solution.py:266
  16.3 0.0 copy-done
  16.3 0.0 copy-done.1
  16.3 0.8 %multiply_add_fusion = (f32[3,16,512]{2,1,0:T(8,128)}, f32[3,16,512]{2,1,0:T(8,128)}) fusion(f32[3,16,512]{2,1,0:T(8,128)S(1)} %get-tuple-element.4, f32[3]{0:T(128)S(1)} %copy-done.1, f32[16,512]{1,0:T(8,128)S(1)} %get-tuple-element.5, f32[3]{0:T(128)S(1)} %copy-done), kind=kLoop, calls=%fused_computation | loop fusion | flops 73728 | bytes 327704 | tf_op jit(solution)/shard_map/add | solution.py:285
Async XLA Ops:
  0.6 15.6 %copy-start = (f32[3]{0:T(128)S(1)}, f32[3]{0:T(128)}, u32[]{:S(2)}) copy-start(f32[3]{0:T(128)} %extinction_in.1) | copy-start | bytes 40
  0.6 15.6 %copy-start.1 = (f32[3]{0:T(128)S(1)}, f32[3]{0:T(128)}, u32[]{:S(2)}) copy-start(f32[3]{0:T(128)} %param.7) | copy-start | bytes 40
